TPU v7x, 512 devices: a whole 4x4x16 slice. The times are simulated.
512 devices in a mesh: dp: 32 (over x, z_hi, core), tensor: 16 (over y, z_lo).
Axes of the slice: x: 4, y: 4, z: 16 (z_hi: 4, z_lo: 4; z = z_hi * 4 + z_lo), core: 2. Of those that a mesh axis runs over, the one named last changes fastest.
Arguments:
- rm_hidden: bfloat16 [32, 1024, 3584], P('dp', 'tensor'), may hold values from -6 to 6
- rm_cotangent: bfloat16 [32, 1024, 3584], P('dp', 'tensor'), may hold values from -6 to 6
- rm_gain: float32 [3584], replicated, may hold values from 0.25 to 1.75
- rewards: float32 [32], P('dp'), may hold values from 0.25 to 8, as said below
- visual_pos: int32 [32, 512], P('dp', 'tensor'), may hold values from 0 to 1023, as said below
- bridge: bfloat16 [3584, 2048], P(None, 'tensor'), may hold values from -0.09375 to 0.09375
- img_query: bfloat16 [32, 2048, 2048], P('dp', 'tensor'), may hold values from -8 to 8
- img_key: bfloat16 [32, 2048, 2048], P('dp', 'tensor'), may hold values from -8 to 8
- img_value: bfloat16 [32, 2048, 2048], P('dp', 'tensor'), may hold values from -6 to 6
Outputs:
- grad_query: bfloat16 [32, 2048, 2048], P('dp', 'tensor')
- grad_key: bfloat16 [32, 2048, 2048], P('dp', 'tensor')
- grad_value: bfloat16 [32, 2048, 2048], P('dp', 'tensor')
Inputs may be any that keep to these rules, and one draw needn't show every extreme that they name: `visual_pos`: strictly increasing in each sample; rows 64 * t to 64 * t + 63 of a reward sequence hold exactly 32 visual tokens, for every t. `rewards`: positive.
All inputs are finite; a program needn't handle non-finite values.
Results may differ from a plain program's by a relative error of at most 0.0082.
Values may be sent and summed in bfloat16 or wider, within the bound.
A program may use at most 64 MiB of HBM per device.

v0:
```python
import functools

import jax
import jax.numpy as jnp
from jax import lax
from jax.sharding import Mesh
from jax.sharding import PartitionSpec as P

HD = 128
GW = 64
DP = ("dp_0", "dp_1", "dp_2")


def one_axis_at_a_time(array, axes):
    return functools.reduce(lax.psum, axes, array)


def norm_backward(hidden, cotangent, gain):
    hidden_f = hidden.astype(jnp.float32)
    scaled_cot = cotangent.astype(jnp.float32) * gain
    inv_rms = lax.rsqrt(jnp.mean(hidden_f * hidden_f, axis=-1, keepdims=True) + 1e-06)
    mixed = jnp.mean(hidden_f * scaled_cot, axis=-1, keepdims=True)
    return (inv_rms * scaled_cot - hidden_f * inv_rms * inv_rms * inv_rms * mixed).astype(
        jnp.bfloat16
    )


def upsample(handed):
    half_width = GW // 2
    grid_rows = handed.reshape(handed.shape[0] // half_width, half_width, handed.shape[1])
    grid_rows = jnp.repeat(jnp.repeat(grid_rows, 2, axis=0), 2, axis=1)
    return grid_rows.reshape(-1, handed.shape[1])


def attend_back(query_rows, key_rows, value_rows, grad_rows):
    seq_length = query_rows.shape[0]
    block_rows = min(512, seq_length)
    score_scale = query_rows.shape[1] ** (-0.5)

    def step(carry, block_index):
        grad_key, grad_value = carry
        first_row = block_index * block_rows
        query_block = lax.dynamic_slice_in_dim(query_rows, first_row, block_rows, 0)
        grad_block = lax.dynamic_slice_in_dim(grad_rows, first_row, block_rows, 0)
        scores = jnp.dot(query_block, key_rows.T, preferred_element_type=jnp.float32) * score_scale
        row_max = jnp.max(scores, axis=1, keepdims=True)
        exp_scores = jnp.exp(scores - row_max)
        attn_weights = exp_scores / jnp.sum(exp_scores, axis=1, keepdims=True)
        weights_half = attn_weights.astype(jnp.bfloat16)
        grad_weights = jnp.dot(grad_block, value_rows.T, preferred_element_type=jnp.float32)
        row_dot = jnp.sum(attn_weights * grad_weights, axis=1, keepdims=True)
        grad_scores = (attn_weights * (grad_weights - row_dot)).astype(jnp.bfloat16)
        grad_query = (
            jnp.dot(grad_scores, key_rows, preferred_element_type=jnp.float32) * score_scale
        ).astype(jnp.bfloat16)
        grad_key = grad_key + jnp.dot(
            grad_scores.T, query_block, preferred_element_type=jnp.float32
        )
        grad_value = grad_value + jnp.dot(
            weights_half.T, grad_block, preferred_element_type=jnp.float32
        )
        return ((grad_key, grad_value), grad_query)

    zeros_init = jnp.zeros(query_rows.shape, jnp.float32)
    carry, query_blocks = lax.scan(
        step, (zeros_init, zeros_init), jnp.arange(seq_length // block_rows, dtype=jnp.int32)
    )
    grad_query = query_blocks.reshape(seq_length, -1)
    grad_key = (carry[0] * score_scale).astype(jnp.bfloat16)
    grad_value = carry[1].astype(jnp.bfloat16)
    return (grad_query, grad_key, grad_value)


def heads_backward(query_rows, key_rows, value_rows, grad_rows):
    seq_length = query_rows.shape[0]
    head_count = query_rows.shape[1] // HD

    def split_heads(array):
        return array.reshape(seq_length, head_count, HD).transpose(1, 0, 2)

    def per_head(head_items):
        return attend_back(head_items[0], head_items[1], head_items[2], head_items[3])

    head_grads = lax.map(
        per_head,
        (
            split_heads(query_rows),
            split_heads(key_rows),
            split_heads(value_rows),
            split_heads(grad_rows),
        ),
    )
    return tuple(
        (grads.transpose(1, 0, 2).reshape(seq_length, head_count * HD) for grads in head_grads)
    )


def local(
    rm_hidden, rm_cotangent, rm_gain, rewards, visual_pos, bridge, img_query, img_key, img_value
):
    reward_sum = one_axis_at_a_time(jnp.sum(rewards), DP)
    sample_count = lax.axis_size(DP) * rewards.shape[0]
    reward_weight = rewards[0] * sample_count / reward_sum
    row_offset = lax.axis_index("tensor") * rm_hidden.shape[1]
    local_rows = visual_pos[0] - row_offset
    vis_hidden = jnp.take(rm_hidden[0], local_rows, axis=0)
    vis_cot = jnp.take(rm_cotangent[0], local_rows, axis=0)
    visual_grad = norm_backward(vis_hidden, vis_cot, rm_gain)
    handed = (
        jnp.dot(
            lax.all_gather(visual_grad, "tensor", axis=0, tiled=True),
            bridge,
            preferred_element_type=jnp.float32,
        )
        * reward_weight
    ).astype(jnp.bfloat16)
    grad_rows = upsample(handed)
    head_query, head_key, head_value = (
        lax.all_to_all(img_query[0], "tensor", split_axis=1, concat_axis=0, tiled=True),
        lax.all_to_all(img_key[0], "tensor", split_axis=1, concat_axis=0, tiled=True),
        lax.all_to_all(img_value[0], "tensor", split_axis=1, concat_axis=0, tiled=True),
    )
    head_grads = heads_backward(head_query, head_key, head_value, grad_rows)
    token_query, token_key, token_value = (
        lax.all_to_all(head_grads[0], "tensor", split_axis=0, concat_axis=1, tiled=True),
        lax.all_to_all(head_grads[1], "tensor", split_axis=0, concat_axis=1, tiled=True),
        lax.all_to_all(head_grads[2], "tensor", split_axis=0, concat_axis=1, tiled=True),
    )
    return (token_query[None], token_key[None], token_value[None])


def solution(mesh):
    torus = Mesh(
        mesh.devices.reshape(4, 4, 2, mesh.shape["tensor"]), ("dp_0", "dp_1", "dp_2", "tensor")
    )
    in_specs = (
        P(DP, "tensor", None),
        P(DP, "tensor", None),
        P(),
        P(DP),
        P(DP, "tensor"),
        P(None, "tensor"),
        P(DP, "tensor", None),
        P(DP, "tensor", None),
        P(DP, "tensor", None),
    )
    out_specs = (P(DP, "tensor", None), P(DP, "tensor", None), P(DP, "tensor", None))
    return jax.shard_map(local, mesh=torus, in_specs=in_specs, out_specs=out_specs, check_vma=False)
```

profile of v0, /device:TPU:6, one launch (start us, length us, event | category | flops | bytes accessed | tf_op | source)
XLA Modules:
  0.0 268.2 jit_solution(7245636634787149169)
XLA Ops:
  8.0 2.0 gather_fusion
  10.1 2.0 gather_fusion.1
  15.2 8.6 %all-to-all-start = ((bf16[128,16,128]{2,0,1:T(8,128)(2,1)}), bf16[128,16,128]{2,0,1:T(8,128)(2,1)S(1)}, u32[]{:S(2)}, u32[]{:S(2)}) async-start(bf16[128,16,128]{2,0,1:T(8,128)(2,1)} %copy.21), calls=%async_computation | async-start | bytes 1048576 | tf_op jit(solution)/shard_map/all_to_all | solution.py:119
  24.9 15.8 %all-to-all-done = bf16[128,16,128]{2,0,1:T(8,128)(2,1)S(1)} async-done(((bf16[128,16,128]{2,0,1:T(8,128)(2,1)}), bf16[128,16,128]{2,0,1:T(8,128)(2,1)S(1)}, u32[]{:S(2)}, u32[]{:S(2)}) %all-to-all-start) | async-done | bytes 524320 | tf_op jit(solution)/shard_map/all_to_all | solution.py:119
  40.7 4.0 %all-to-all-start.2 = ((bf16[128,16,128]{2,0,1:T(8,128)(2,1)}), bf16[128,16,128]{2,0,1:T(8,128)(2,1)S(1)}, u32[]{:S(2)}, u32[]{:S(2)}) async-start(bf16[128,16,128]{2,0,1:T(8,128)(2,1)} %copy.23), calls=%async_computation.2 | async-start | bytes 1048576 | tf_op jit(solution)/shard_map/all_to_all | solution.py:121
  45.8 29.3 %all-to-all-done.2 = bf16[128,16,128]{2,0,1:T(8,128)(2,1)S(1)} async-done(((bf16[128,16,128]{2,0,1:T(8,128)(2,1)}), bf16[128,16,128]{2,0,1:T(8,128)(2,1)S(1)}, u32[]{:S(2)}, u32[]{:S(2)}) %all-to-all-start.2) | async-done | bytes 524320 | tf_op jit(solution)/shard_map/all_to_all | solution.py:121
  75.1 3.6 %all-to-all-start.1 = ((bf16[128,16,128]{2,0,1:T(8,128)(2,1)}), bf16[128,16,128]{2,0,1:T(8,128)(2,1)S(1)}, u32[]{:S(2)}, u32[]{:S(2)}) async-start(bf16[128,16,128]{2,0,1:T(8,128)(2,1)} %copy.22), calls=%async_computation.1 | async-start | bytes 1048576 | tf_op jit(solution)/shard_map/all_to_all | solution.py:120
  78.7 8.1 %psum.21 = f32[]{:T(128)} all-reduce(f32[]{:T(128)} %bitcast.7), channel_id=1, replica_groups=mesh['dp_0'=4,'dp_1'=4,'dp_2'=2,'tensor'=16] {'dp_0'}, use_global_device_ids=true, to_apply=%region_2.4 | all-reduce | flops 1 | bytes 8 | tf_op jit(solution)/shard_map/psum | solution.py:15
  86.8 26.3 %psum.22 = f32[]{:T(128)} all-reduce(f32[]{:T(128)} %psum.21), channel_id=1, replica_groups=mesh['dp_0'=4,'dp_1'=4,'dp_2'=2,'tensor'=16] {'dp_1'}, use_global_device_ids=true, to_apply=%region_3.5 | all-reduce | flops 1 | bytes 8 | tf_op jit(solution)/shard_map/psum | solution.py:15
  113.1 3.1 %psum.23 = f32[]{:T(128)} all-reduce(f32[]{:T(128)} %psum.22), channel_id=1, replica_groups=mesh['dp_0'=4,'dp_1'=4,'dp_2'=2,'tensor'=16] {'dp_2'}, use_global_device_ids=true, to_apply=%region_4.0 | all-reduce | flops 1 | bytes 8 | tf_op jit(solution)/shard_map/psum | solution.py:15
  117.6 21.0 %all-gather.2.cloned.1.call-done = bf16[512,3584]{1,0:T(8,128)(2,1)} async-done(((bf16[32,3584]{1,0:T(8,128)(2,1)}), bf16[512,3584]{1,0:T(8,128)(2,1)}) %all-gather.2.cloned.1.call-update) | async-done | bytes 3670032 | tf_op jit(solution)/shard_map/all_gather | solution.py:111
  138.5 3.1 %fusion.17 = bf16[512,128]{1,0:T(8,128)(2,1)S(1)} fusion(bf16[512,3584]{1,0:T(8,128)(2,1)} %all-gather.2.cloned.1.call-done, bf16[3584,128]{1,0:T(8,128)(2,1)S(1)} %copy-done, f32[]{:T(128)S(6)} %div.19), kind=kOutput, calls=%fused_computation.26 | convolution fusion | flops 469893120 | bytes 4718596 | tf_op jit(solution)/shard_map/dot_general | solution.py:110
  142.2 60.4 %while.26 = (s32[]{:T(128)}, f32[2048,128]{1,0:T(8,128)S(1)}, f32[2048,128]{1,0:T(8,128)}, bf16[4,512,128]{2,1,0:T(8,128)(2,1)}, s32[4]{0:T(128)S(1)}, /*index=5...) while((s32[]{:T(128)}, f32[2048,128]{1,0:T(8,128)S(1)}, ...), condition=%wide.region_9.11_spmd.clone, body=%wide.region_5.10_spmd.clone.sunk | while | flops 1364326912 | bytes 77749032 | solution.py:65
  144.3 1.9 copy-done.1
  147.0 4.5 %convolution_add_fusion.5 = f32[2048,128]{1,0:T(8,128)} fusion(f32[2048,128]{1,0:T(8,128)} %get-tuple-element.219, pred[]{:T(512)S(6)} %compare.3, bf16[2048,128]{1,0:T(8,128)(2,1)S(1)} %get-tuple-element.237, s32[]{:T(128)S(6)} %select_n.33, f32[512,2048]{1,0:T(8,128)} %copy-done.1, f32[512]{0:T(512)S(1)} %fusion.50, f32[512]{0:T(512)S(1)} %get-tuple-element.201), kind=kOutput, calls=%fused_computation.8.clone.1 | convolution fusion | flops 273154048 | bytes 6426629 | tf_op jit(solution)/shard_map/while/body/eval_jaxpr/while/body/eval_jaxpr/dot_general | solution.py:59
  159.1 1.9 copy-done.1
  161.9 4.8 %convolution_add_fusion.5 = f32[2048,128]{1,0:T(8,128)} fusion(f32[2048,128]{1,0:T(8,128)} %get-tuple-element.219, pred[]{:T(512)S(6)} %compare.3, bf16[2048,128]{1,0:T(8,128)(2,1)S(1)} %get-tuple-element.237, s32[]{:T(128)S(6)} %select_n.33, f32[512,2048]{1,0:T(8,128)} %copy-done.1, f32[512]{0:T(512)S(1)} %fusion.50, f32[512]{0:T(512)S(1)} %get-tuple-element.201), kind=kOutput, calls=%fused_computation.8.clone.1 | convolution fusion | flops 273154048 | bytes 6426629 | tf_op jit(solution)/shard_map/while/body/eval_jaxpr/while/body/eval_jaxpr/dot_general | solution.py:59
  177.1 4.8 %convolution_add_fusion.5 = f32[2048,128]{1,0:T(8,128)} fusion(f32[2048,128]{1,0:T(8,128)} %get-tuple-element.219, pred[]{:T(512)S(6)} %compare.3, bf16[2048,128]{1,0:T(8,128)(2,1)S(1)} %get-tuple-element.237, s32[]{:T(128)S(6)} %select_n.33, f32[512,2048]{1,0:T(8,128)} %copy-done.1, f32[512]{0:T(512)S(1)} %fusion.50, f32[512]{0:T(512)S(1)} %get-tuple-element.201), kind=kOutput, calls=%fused_computation.8.clone.1 | convolution fusion | flops 273154048 | bytes 6426629 | tf_op jit(solution)/shard_map/while/body/eval_jaxpr/while/body/eval_jaxpr/dot_general | solution.py:59
  192.3 4.8 %convolution_add_fusion.5 = f32[2048,128]{1,0:T(8,128)} fusion(f32[2048,128]{1,0:T(8,128)} %get-tuple-element.219, pred[]{:T(512)S(6)} %compare.3, bf16[2048,128]{1,0:T(8,128)(2,1)S(1)} %get-tuple-element.237, s32[]{:T(128)S(6)} %select_n.33, f32[512,2048]{1,0:T(8,128)} %copy-done.1, f32[512]{0:T(512)S(1)} %fusion.50, f32[512]{0:T(512)S(1)} %get-tuple-element.201), kind=kOutput, calls=%fused_computation.8.clone.1 | convolution fusion | flops 273154048 | bytes 6426629 | tf_op jit(solution)/shard_map/while/body/eval_jaxpr/while/body/eval_jaxpr/dot_general | solution.py:59
  203.5 4.8 %all-to-all-start.4 = ((bf16[16,128,128]{2,1,0:T(8,128)(2,1)}), bf16[16,128,128]{2,1,0:T(8,128)(2,1)S(1)}, u32[]{:S(2)}, u32[]{:S(2)}) async-start(bf16[16,128,128]{2,1,0:T(8,128)(2,1)} %bitcast.16), calls=%async_computation.4 | async-start | bytes 1048576 | tf_op jit(solution)/shard_map/all_to_all | solution.py:126
  209.7 13.2 %all-to-all-done.4 = bf16[16,128,128]{2,1,0:T(8,128)(2,1)S(1)} async-done(((bf16[16,128,128]{2,1,0:T(8,128)(2,1)}), bf16[16,128,128]{2,1,0:T(8,128)(2,1)S(1)}, u32[]{:S(2)}, u32[]{:S(2)}) %all-to-all-start.4) | async-done | bytes 524320 | tf_op jit(solution)/shard_map/all_to_all | solution.py:126
  222.9 18.2 %all_to_all.96 = bf16[16,128,128]{2,1,0:T(8,128)(2,1)S(1)} all-to-all(bf16[16,128,128]{2,1,0:T(8,128)(2,1)S(1)} %bitcast.70), channel_id=1, replica_groups=mesh['dp_0'=4,'dp_1'=4,'dp_2'=2,'tensor'=16] {'tensor'}, dimensions={0} | all-to-all | bytes 1048576 | tf_op jit(solution)/shard_map/all_to_all | solution.py:127
  241.1 3.6 %all-to-all-start.3 = ((bf16[16,128,128]{2,1,0:T(8,128)(2,1)}), bf16[16,128,128]{2,1,0:T(8,128)(2,1)S(1)}, u32[]{:S(2)}, u32[]{:S(2)}) async-start(bf16[16,128,128]{2,1,0:T(8,128)(2,1)} %bitcast.13), calls=%async_computation.3 | async-start | bytes 1048576 | tf_op jit(solution)/shard_map/all_to_all | solution.py:125
  247.2 12.8 %all-to-all-done.3 = bf16[16,128,128]{2,1,0:T(8,128)(2,1)S(1)} async-done(((bf16[16,128,128]{2,1,0:T(8,128)(2,1)}), bf16[16,128,128]{2,1,0:T(8,128)(2,1)S(1)}, u32[]{:S(2)}, u32[]{:S(2)}) %all-to-all-start.3) | async-done | bytes 524320 | tf_op jit(solution)/shard_map/all_to_all | solution.py:125
  (90 shorter events, 47.3 us)
Async XLA Ops:
  7.2 131.4 %copy-start = (bf16[3584,128]{1,0:T(8,128)(2,1)S(1)}, bf16[3584,128]{1,0:T(8,128)(2,1)}, u32[]{:S(2)}) copy-start(bf16[3584,128]{1,0:T(8,128)(2,1)} %param.18) | copy-start | bytes 2752516
  7.2 6.0 %copy-start.8 = (f32[3584]{0:T(1024)S(1)}, f32[3584]{0:T(1024)}, u32[]{:S(2)}) copy-start(f32[3584]{0:T(1024)} %param.15) | copy-start | bytes 43012
  7.2 7.0 %copy-start.3 = (bf16[1,128,2048]{2,1,0:T(8,128)(2,1)S(1)}, bf16[1,128,2048]{2,1,0:T(8,128)(2,1)}, u32[]{:S(2)}) copy-start(bf16[1,128,2048]{2,1,0:T(8,128)(2,1)} %param.19) | copy-start | bytes 1572868
  7.2 131.3 %all-gather.2.cloned.1.call-start = ((), (), s32[]{:S(2)}) async-start(), calls=%async_computation.6 | async-start | bytes 3899392 | tf_op jit(solution)/shard_map/all_gather | solution.py:111
  8.0 15.8 %copy-start.4 = (bf16[1,128,2048]{2,1,0:T(8,128)(2,1)S(1)}, bf16[1,128,2048]{2,1,0:T(8,128)(2,1)}, u32[]{:S(2)}) copy-start(bf16[1,128,2048]{2,1,0:T(8,128)(2,1)} %param.21) | copy-start | bytes 1572868
  12.1 32.7 %copy-start.5 = (bf16[1,128,2048]{2,1,0:T(8,128)(2,1)S(1)}, bf16[1,128,2048]{2,1,0:T(8,128)(2,1)}, u32[]{:S(2)}) copy-start(bf16[1,128,2048]{2,1,0:T(8,128)(2,1)} %param.20) | copy-start | bytes 1572868
  15.2 25.5 %all-to-all-start = ((bf16[128,16,128]{2,0,1:T(8,128)(2,1)}), bf16[128,16,128]{2,0,1:T(8,128)(2,1)S(1)}, u32[]{:S(2)}, u32[]{:S(2)}) async-start(bf16[128,16,128]{2,0,1:T(8,128)(2,1)} %copy.21), calls=%async_computation | async-start | bytes 1048576 | tf_op jit(solution)/shard_map/all_to_all | solution.py:119
  40.7 34.4 %all-to-all-start.2 = ((bf16[128,16,128]{2,0,1:T(8,128)(2,1)}), bf16[128,16,128]{2,0,1:T(8,128)(2,1)S(1)}, u32[]{:S(2)}, u32[]{:S(2)}) async-start(bf16[128,16,128]{2,0,1:T(8,128)(2,1)} %copy.23), calls=%async_computation.2 | async-start | bytes 1048576 | tf_op jit(solution)/shard_map/all_to_all | solution.py:121
  75.1 41.1 %copy-start.6 = (bf16[128,16,128]{2,0,1:T(8,128)(2,1)}, bf16[128,16,128]{2,0,1:T(8,128)(2,1)S(1)}, u32[]{:S(2)}) copy-start(bf16[128,16,128]{2,0,1:T(8,128)(2,1)S(1)} %all-to-all-done.2) | copy-start | bytes 1572868
  75.1 66.6 %all-to-all-start.1 = ((bf16[128,16,128]{2,0,1:T(8,128)(2,1)}), bf16[128,16,128]{2,0,1:T(8,128)(2,1)S(1)}, u32[]{:S(2)}, u32[]{:S(2)}) async-start(bf16[128,16,128]{2,0,1:T(8,128)(2,1)} %copy.22), calls=%async_computation.1 | async-start | bytes 1048576 | tf_op jit(solution)/shard_map/all_to_all | solution.py:120
  144.3 1.9 copy-start.1
  147.0 4.6 %copy-start.2 = (f32[512,2048]{1,0:T(8,128)S(1)}, f32[512,2048]{1,0:T(8,128)}, u32[]{:S(2)}) copy-start(f32[512,2048]{1,0:T(8,128)} %copy-done.1) | copy-start | bytes 12582916 | tf_op jit(solution)/shard_map/while/body/eval_jaxpr/while
  147.0 4.6 %copy-start.7 = (bf16[2048,128]{1,0:T(8,128)(2,1)S(1)}, bf16[2048,128]{1,0:T(8,128)(2,1)}, u32[]{:S(2)}) copy-start(bf16[2048,128]{1,0:T(8,128)(2,1)} %get-tuple-element.238) | copy-start | bytes 1572868 | tf_op jit(solution)/shard_map/while/body/eval_jaxpr/while
  159.1 1.9 copy-start.1
  161.9 4.9 %copy-start.2 = (f32[512,2048]{1,0:T(8,128)S(1)}, f32[512,2048]{1,0:T(8,128)}, u32[]{:S(2)}) copy-start(f32[512,2048]{1,0:T(8,128)} %copy-done.1) | copy-start | bytes 12582916 | tf_op jit(solution)/shard_map/while/body/eval_jaxpr/while
  161.9 4.8 %copy-start.7 = (bf16[2048,128]{1,0:T(8,128)(2,1)S(1)}, bf16[2048,128]{1,0:T(8,128)(2,1)}, u32[]{:S(2)}) copy-start(bf16[2048,128]{1,0:T(8,128)(2,1)} %get-tuple-element.238) | copy-start | bytes 1572868 | tf_op jit(solution)/shard_map/while/body/eval_jaxpr/while
  174.3 1.9 copy-start.1
  177.1 4.9 %copy-start.2 = (f32[512,2048]{1,0:T(8,128)S(1)}, f32[512,2048]{1,0:T(8,128)}, u32[]{:S(2)}) copy-start(f32[512,2048]{1,0:T(8,128)} %copy-done.1) | copy-start | bytes 12582916 | tf_op jit(solution)/shard_map/while/body/eval_jaxpr/while
  177.1 4.8 %copy-start.7 = (bf16[2048,128]{1,0:T(8,128)(2,1)S(1)}, bf16[2048,128]{1,0:T(8,128)(2,1)}, u32[]{:S(2)}) copy-start(bf16[2048,128]{1,0:T(8,128)(2,1)} %get-tuple-element.238) | copy-start | bytes 1572868 | tf_op jit(solution)/shard_map/while/body/eval_jaxpr/while
  189.5 1.9 copy-start.1
  192.3 4.9 %copy-start.2 = (f32[512,2048]{1,0:T(8,128)S(1)}, f32[512,2048]{1,0:T(8,128)}, u32[]{:S(2)}) copy-start(f32[512,2048]{1,0:T(8,128)} %copy-done.1) | copy-start | bytes 12582916 | tf_op jit(solution)/shard_map/while/body/eval_jaxpr/while
  192.3 4.8 %copy-start.7 = (bf16[2048,128]{1,0:T(8,128)(2,1)S(1)}, bf16[2048,128]{1,0:T(8,128)(2,1)}, u32[]{:S(2)}) copy-start(bf16[2048,128]{1,0:T(8,128)(2,1)} %get-tuple-element.238) | copy-start | bytes 1572868 | tf_op jit(solution)/shard_map/while/body/eval_jaxpr/while
  203.5 19.3 %all-to-all-start.4 = ((bf16[16,128,128]{2,1,0:T(8,128)(2,1)}), bf16[16,128,128]{2,1,0:T(8,128)(2,1)S(1)}, u32[]{:S(2)}, u32[]{:S(2)}) async-start(bf16[16,128,128]{2,1,0:T(8,128)(2,1)} %bitcast.16), calls=%async_computation.4 | async-start | bytes 1048576 | tf_op jit(solution)/shard_map/all_to_all | solution.py:126
  241.1 19.0 %all-to-all-start.3 = ((bf16[16,128,128]{2,1,0:T(8,128)(2,1)}), bf16[16,128,128]{2,1,0:T(8,128)(2,1)S(1)}, u32[]{:S(2)}, u32[]{:S(2)}) async-start(bf16[16,128,128]{2,1,0:T(8,128)(2,1)} %bitcast.13), calls=%async_computation.3 | async-start | bytes 1048576 | tf_op jit(solution)/shard_map/all_to_all | solution.py:125
Sparse Core Ops, SparseCore 0:
  14.3 124.2 all-gather.1
where the time goes:
time: 270 us; the launch traced here: 268 us
  waiting for transfers between devices  92 us (34%)
  blocking collectives  55.7 us (21%)
  matrix products  41.8 us (15%)
  starting transfers between devices  24.7 us (9%)
  local copies, waits for them, and re-layouts  21.7 us (8%)
  between operations  15.6 us (6%)
  other arithmetic  13.8 us (5%)
  loops' own time  2.84 us (1%)
    psum x3, blocking collectives, one_axis_at_a_time(): return functools.reduce(lax.psum, axes, array)  37.6 us
    all_to_all x1, waiting for transfers between devices, local(): lax.all_to_all(img_value[0], 'tensor', split_axis=1, concat_axis=0, tiled...  29.3 us
    all_gather x1, waiting for transfers between devices, local(): lax.all_gather(visual_grad, 'tensor', axis=0, tiled=True)  21 us
    dot_general x4, matrix products, step(): jnp.dot(weights_half.T, grad_block, preferred_element_type=jnp.float32)  19 us
    all_to_all x1, blocking collectives, local(): lax.all_to_all(head_grads[2], 'tensor', split_axis=0, concat_axis=1, tile...  18.2 us
    all_to_all x1, waiting for transfers between devices, local(): lax.all_to_all(img_query[0], 'tensor', split_axis=1, concat_axis=0, tiled...  15.8 us
    all_to_all x1, waiting for transfers between devices, local(): lax.all_to_all(head_grads[1], 'tensor', split_axis=0, concat_axis=1, tile...  13.2 us
    all_to_all x1, waiting for transfers between devices, local(): lax.all_to_all(head_grads[0], 'tensor', split_axis=0, concat_axis=1, tile...  12.8 us
  transfers between devices with their start and end apart: 6, of which 5 were waited for; matrix products, arithmetic and copies ran while one was open for 4% of the time, Pallas kernels for 0%

commit v1 on v0

v1 whole, which is shorter than its diff:
```python
import functools
from typing import NamedTuple, Any

import jax
import jax.numpy as jnp
from jax import lax
from jax.experimental import pallas as pl
from jax.experimental.pallas import tpu as pltpu
from jax.sharding import Mesh
from jax.sharding import PartitionSpec as P

HD = 128
GW = 64
D = 3584
DP = ("dp_0", "dp_1", "dp_2")
SEQ = 2048
VIS = 512
TP = 16
NY, NZ = 4, 4
QB = 512
UB = QB // 4
KC = 256
SCALE = HD**-0.5
LOG2E = 1.4426950408889634
BF = jnp.bfloat16
F32 = jnp.float32

NT = (((1,), (1,)), ((), ()))
NN = (((1,), (0,)), ((), ()))
TN = (((0,), (0,)), ((), ()))


def mm(a, b, dims=NN):
    return lax.dot_general(a, b, dims, preferred_element_type=F32)


class AttnScratch(NamedTuple):
    s_buf: Any
    dp_buf: Any
    perm: Any
    perm_t: Any
    k_t: Any
    dq_t: Any
    dk_acc: Any
    dv_acc: Any


def attn_scratch():
    return [
        pltpu.VMEM((SEQ, QB), F32),
        pltpu.VMEM((SEQ, UB), F32),
        pltpu.VMEM((QB, QB), BF),
        pltpu.VMEM((QB, QB), BF),
        pltpu.VMEM((HD, SEQ), BF),
        pltpu.VMEM((HD, QB), F32),
        pltpu.VMEM((SEQ, HD), F32),
        pltpu.VMEM((SEQ, HD), F32),
    ]


def grouped(rank):
    group, place = rank // UB, rank % UB
    return (place // 32) * HD + (group // 2) * GW + 2 * (place % 32) + group % 2


def attn_tables(env):
    row = lax.broadcasted_iota(jnp.int32, (QB, QB), 0)
    col = lax.broadcasted_iota(jnp.int32, (QB, QB), 1)
    env.perm[...] = (grouped(row) == col).astype(F32).astype(BF)
    env.perm_t[...] = (grouped(col) == row).astype(F32).astype(BF)
    env.dk_acc[...] = jnp.zeros((SEQ, HD), F32)
    env.dv_acc[...] = jnp.zeros((SEQ, HD), F32)


def attn_transpose(env, k_all):
    eye = (
        lax.broadcasted_iota(jnp.int32, (HD, HD), 0)
        == lax.broadcasted_iota(jnp.int32, (HD, HD), 1)
    ).astype(F32).astype(BF)
    env.k_t[...] = mm(eye, k_all[...], NT).astype(BF)


def attn_setup(env, k_all):
    attn_tables(env)
    attn_transpose(env, k_all)


def fold(values, op):
    return op(values.reshape(values.shape[0] // 8, 8, values.shape[1]), axis=0)


def four(values):
    return jnp.concatenate([values] * 4, axis=1)


def attn_block(env, block, q_all, k_all, v_all, hand_all, dq_all):
    q_rows = pl.ds(pl.multiple_of(block * QB, QB), QB)
    q_g = mm(env.perm[...], q_all[q_rows, :]).astype(BF)
    hand = hand_all[pl.ds(pl.multiple_of(block * UB, UB), UB), :]

    def rows(chunk):
        return pl.ds(pl.multiple_of(chunk * KC, KC), KC)

    def scores(chunk, top):
        s = mm(k_all[rows(chunk), :], q_g, NT)
        env.s_buf[rows(chunk), :] = s
        return jnp.maximum(top, fold(s, jnp.max))

    top = lax.fori_loop(0, SEQ // KC, scores, jnp.full((8, QB), -jnp.inf, F32), unroll=2)
    top = jnp.max(top, axis=0, keepdims=True)

    def weights(chunk, carry):
        total, dot_sum = carry
        e = jnp.exp2((env.s_buf[rows(chunk), :] - top) * (SCALE * LOG2E))
        env.s_buf[rows(chunk), :] = e
        dp = mm(v_all[rows(chunk), :], hand, NT)
        env.dp_buf[rows(chunk), :] = dp
        return total + fold(e, jnp.sum), dot_sum + fold(e * four(dp), jnp.sum)

    zeros = jnp.zeros((8, QB), F32)
    total, dot_sum = lax.fori_loop(0, SEQ // KC, weights, (zeros, zeros), unroll=2)
    inv = 1.0 / jnp.sum(total, axis=0, keepdims=True)
    row_dot = jnp.sum(dot_sum, axis=0, keepdims=True) * inv
    env.dq_t[...] = jnp.zeros((HD, QB), F32)

    def grads(chunk, _):
        p = env.s_buf[rows(chunk), :] * inv
        ds = (p * (four(env.dp_buf[rows(chunk), :]) - row_dot)).astype(BF)
        p_sum = (p[:, :UB] + p[:, UB : 2 * UB]) + (p[:, 2 * UB : 3 * UB] + p[:, 3 * UB :])
        env.dk_acc[rows(chunk), :] += mm(ds, q_g)
        env.dv_acc[rows(chunk), :] += mm(p_sum.astype(BF), hand)
        env.dq_t[...] += mm(env.k_t[:, rows(chunk)], ds)
        return 0

    lax.fori_loop(0, SEQ // KC, grads, 0, unroll=2)
    dq_t = (env.dq_t[...] * SCALE).astype(BF)
    dq_all[q_rows, :] = mm(env.perm_t[...], dq_t, NT).astype(BF)


def attn_finish(env, dk_all, dv_all):
    dk_all[...] = (env.dk_acc[...] * SCALE).astype(BF)
    dv_all[...] = env.dv_acc[...].astype(BF)


class Links(NamedTuple):
    x: Any
    z_hi: Any
    core: Any
    tensor: Any
    sizes: tuple


def remote(src, dst, send_sem, recv_sem, device):
    return pltpu.make_async_remote_copy(
        src_ref=src,
        dst_ref=dst,
        send_sem=send_sem,
        recv_sem=recv_sem,
        device_id=device,
        device_id_type=pl.DeviceIdType.MESH,
    )


def kernel(
    sizes,
    rew_ref,
    pos_ref,
    gain_ref,
    hid_hbm,
    cot_hbm,
    bridge_hbm,
    q_hbm,
    k_hbm,
    v_hbm,
    dq_out,
    dk_out,
    dv_out,
    hid,
    cot,
    vg_all,
    bridge_all,
    hand_mine,
    hand_all,
    q_all,
    k_all,
    v_all,
    dq_all,
    dk_all,
    dv_all,
    rew,
    own_sem,
    rew_send,
    rew_recv,
    vg_send,
    vg_recv,
    br_send,
    br_recv,
    hand_send,
    hand_recv,
    q_send,
    q_recv,
    k_send,
    k_recv,
    v_send,
    v_recv,
    dq_send,
    dq_recv,
    dk_send,
    dk_recv,
    dv_send,
    dv_recv,
    *scratch,
):
    env = AttnScratch(*scratch)
    n_x, n_zhi, n_core = sizes
    x, z_hi, core, me = (lax.axis_index(a) for a in (*DP, "tensor"))
    y, z = me // NZ, me % NZ
    axis_of = {"dp_0": (x, n_x), "dp_1": (z_hi, n_zhi), "dp_2": (core, n_core)}

    def turned(name, step):
        place, size = axis_of[name]
        return {name: lax.rem(place + step, size)}

    barrier = pltpu.get_barrier_semaphore()

    def greet(step, _):
        pl.semaphore_signal(
            barrier,
            inc=1,
            device_id={"tensor": lax.rem(me + step, TP)},
            device_id_type=pl.DeviceIdType.MESH,
        )
        return 0

    lax.fori_loop(1, TP, greet, 0)
    partners = TP - 1
    for name, (_, size) in axis_of.items():
        for step in range(1, size):
            pl.semaphore_signal(
                barrier, inc=1, device_id=turned(name, step), device_id_type=pl.DeviceIdType.MESH
            )
            partners += 1

    mine = pl.ds(pl.multiple_of(me * HD, HD), HD)
    my_cols = pl.ds(pl.multiple_of(y * HD, HD), HD)
    local = [
        pltpu.make_async_copy(hid_hbm, hid, own_sem.at[0]),
        pltpu.make_async_copy(cot_hbm, cot, own_sem.at[1]),
        pltpu.make_async_copy(bridge_hbm, bridge_all.at[:, my_cols], own_sem.at[2]),
        pltpu.make_async_copy(k_hbm.at[:, mine], k_all.at[mine, :], own_sem.at[3]),
        pltpu.make_async_copy(v_hbm.at[:, mine], v_all.at[mine, :], own_sem.at[4]),
        pltpu.make_async_copy(q_hbm.at[:, mine], q_all.at[mine, :], own_sem.at[5]),
    ]
    for copy in local:
        copy.start()
    pl.semaphore_wait(barrier, partners)

    def reward_copies(first, name):
        place, size = axis_of[name]
        return [
            remote(
                rew.at[first + place],
                rew.at[first + place],
                rew_send.at[first + step],
                rew_recv.at[first + place],
                turned(name, step),
            )
            for step in range(1, size)
        ]

    def reward_start(first, name, value):
        rew[first + axis_of[name][0]] = value
        for copy in reward_copies(first, name):
            copy.start()

    def reward_sum(first, name):
        place, size = axis_of[name]
        for step in range(1, size):
            other = lax.rem(place + step, size)
            remote(
                rew.at[first + other],
                rew.at[first + other],
                rew_send.at[first + step],
                rew_recv.at[first + other],
                turned(name, step),
            ).wait_recv()
        total = rew[first]
        for slot in range(1, size):
            total = total + rew[first + slot]
        return total

    my_reward = jnp.full((8, HD), rew_ref[0], F32)
    reward_start(0, "dp_2", my_reward)

    half, quarter = D // 2, D // 4
    up, down = {"tensor": lax.rem(y + 1, NY) * NZ + z}, {"tensor": lax.rem(y + NY - 1, NY) * NZ + z}

    def bridge_region(owner, first, count):
        return bridge_all.at[
            pl.ds(pl.multiple_of(first, 16), count),
            pl.ds(pl.multiple_of(owner * HD, HD), HD),
        ]

    def bridge_own(device, slot):
        rows = pl.ds(pl.multiple_of(core * half, 16), half)
        return remote(
            bridge_hbm.at[rows, :],
            bridge_region(y, core * half, half),
            br_send.at[slot],
            br_recv.at[slot],
            device,
        )

    def bridge_copy(owner, first, count, slot, device):
        region = bridge_region(owner, first, count)
        return remote(region, region, br_send.at[slot], br_recv.at[slot], device)

    below, above = lax.rem(y + NY - 1, NY), lax.rem(y + 1, NY)
    across = lax.rem(y + 2, NY)
    bridge_up, bridge_down = bridge_own(up, 0), bridge_own(down, 1)
    bridge_up.start()
    bridge_down.start()

    def peer_at(step):
        d_y, d_z = step // NZ, step % NZ
        return lax.rem(y - d_y + NY, NY) * NZ + lax.rem(z + d_z, NZ)

    def head_send(array, all_ref, sends, recvs, peer):
        cols = pl.ds(pl.multiple_of(peer * HD, HD), HD)
        return remote(
            array.at[:, cols], all_ref.at[mine, :], sends.at[peer], recvs.at[me], {"tensor": peer}
        )

    def head_recv(all_ref, sends, recvs, peer):
        region = all_ref.at[pl.ds(pl.multiple_of(peer * HD, HD), HD), :]
        return remote(region, region, sends.at[peer], recvs.at[peer], {"tensor": peer})

    def to_all(copy_to):
        def one(step, _):
            copy_to(peer_at(step))
            return 0

        lax.fori_loop(1, TP, one, 0)

    to_all(lambda peer: head_send(k_hbm, k_all, k_send, k_recv, peer).start())

    local[0].wait()
    local[1].wait()
    local_rows = pos_ref[...] - me * hid.shape[0]
    picked = (
        lax.broadcasted_iota(jnp.int32, (hid.shape[0], local_rows.shape[1]), 0) == local_rows
    )
    picked = picked.astype(F32).astype(BF)
    hidden = mm(picked, hid[...], TN)
    scaled = mm(picked, cot[...], TN) * gain_ref[...]
    inv_rms = lax.rsqrt(jnp.mean(hidden * hidden, axis=-1, keepdims=True) + 1e-06)
    mixed = jnp.mean(hidden * scaled, axis=-1, keepdims=True)
    count = local_rows.shape[1]
    vg_all[pl.ds(pl.multiple_of(z * count, count), count), :] = (
        inv_rms * scaled - hidden * (inv_rms * inv_rms * inv_rms * mixed)
    ).astype(BF)

    def vg_copy(owner, slot, device):
        region = vg_all.at[pl.ds(pl.multiple_of(owner * count, count), count), :]
        return remote(region, region, vg_send.at[slot], vg_recv.at[slot], device)

    right = {"tensor": y * NZ + lax.rem(z + 1, NZ)}
    left = {"tensor": y * NZ + lax.rem(z + NZ - 1, NZ)}

    def vg_hop(hop, action):
        @pl.when((z < NZ - 1) & (z >= hop))
        def _():
            action(vg_copy(lax.rem(z - hop + NZ, NZ), hop, right))

        @pl.when((z > 0) & (z + hop < NZ))
        def _():
            action(vg_copy(lax.rem(z + hop, NZ), NZ + hop, left))

    def vg_take(hop):
        @pl.when(z > hop)
        def _():
            vg_copy(lax.rem(z - hop - 1 + NZ, NZ), hop, left).wait_recv()

        @pl.when(z + hop + 1 < NZ)
        def _():
            vg_copy(lax.rem(z + hop + 1, NZ), NZ + hop, right).wait_recv()

    vg_hop(0, lambda copy: copy.start())
    to_all(lambda peer: head_send(v_hbm, v_all, v_send, v_recv, peer).start())
    core_total = reward_sum(0, "dp_2")
    reward_start(2, "dp_0", core_total)
    attn_tables(env)

    vg_take(0)
    vg_hop(1, lambda copy: copy.start())
    to_all(lambda peer: head_send(q_hbm, q_all, q_send, q_recv, peer).start())
    x_total = reward_sum(2, "dp_0")
    reward_start(2 + 4, "dp_1", x_total)

    sibling = turned("dp_2", 1)
    bridge_copy(below, core * half, half, 0, down).wait_recv()
    on_up = bridge_copy(below, core * half, quarter, 2, up)
    on_up.start()
    share_below = bridge_copy(below, core * half, half, 4, sibling)
    share_below.start()
    bridge_copy(above, core * half, half, 1, up).wait_recv()
    on_down = bridge_copy(above, core * half + quarter, quarter, 3, down)
    on_down.start()
    share_above = bridge_copy(above, core * half, half, 5, sibling)
    share_above.start()
    vg_take(1)
    vg_hop(2, lambda copy: copy.start())
    bridge_copy(across, core * half, quarter, 2, down).wait_recv()
    bridge_copy(across, core * half + quarter, quarter, 3, up).wait_recv()
    share_across = bridge_copy(across, core * half, half, 6, sibling)
    share_across.start()
    other = (1 - core) * half
    vg_take(2)
    z_total = reward_sum(2 + 4, "dp_1")
    weight = rew_ref[0] * (n_x * n_zhi * n_core) / z_total[0:1, :]

    def hand_head(owner):
        cols = pl.ds(pl.multiple_of(owner * HD, HD), HD)
        product = mm(vg_all[...], bridge_all[:, cols])
        return (product * weight).astype(BF)

    my_rows = pl.ds(pl.multiple_of(y * UB, UB), UB)

    def hand_copy(step):
        head = lax.rem(y + step, NY)
        return remote(
            hand_mine.at[step],
            hand_all.at[my_rows, :],
            hand_send.at[step],
            hand_recv.at[y],
            {"tensor": head * NZ + z},
        )

    local[2].wait()
    hand_all[my_rows, :] = hand_head(y)
    for step, slot in ((1, 5), (3, 4), (2, 6)):
        owner = lax.rem(y + step, NY)
        bridge_copy(owner, other, half, slot, sibling).wait_recv()
        hand_mine[step] = hand_head(owner)
        hand_copy(step).start()

    for copy in local[3:]:
        copy.wait()
    to_all(lambda peer: head_recv(k_all, k_send, k_recv, peer).wait_recv())
    attn_transpose(env, k_all)
    to_all(lambda peer: head_recv(v_all, v_send, v_recv, peer).wait_recv())
    for step in range(1, NY):
        src = lax.rem(y + step, NY)
        region = hand_all.at[pl.ds(pl.multiple_of(src * UB, UB), UB), :]
        remote(
            region, region, hand_send.at[step], hand_recv.at[src], {"tensor": src * NZ + z}
        ).wait_recv()

    def token_send(all_ref, out, sends, recvs, peer):
        rows = pl.ds(pl.multiple_of(peer * HD, HD), HD)
        return remote(
            all_ref.at[rows, :], out.at[:, mine], sends.at[peer], recvs.at[me], {"tensor": peer}
        )

    def token_recv(out, sends, recvs, peer):
        region = out.at[:, pl.ds(pl.multiple_of(peer * HD, HD), HD)]
        return remote(region, region, sends.at[peer], recvs.at[peer], {"tensor": peer})

    def token_own(all_ref, out, slot):
        return pltpu.make_async_copy(all_ref.at[mine, :], out.at[:, mine], own_sem.at[slot])

    def attend(step, _):
        block = lax.rem(y + step, NY)

        def take(i, _):
            peer = block * NZ + i

            @pl.when(peer != me)
            def _():
                head_recv(q_all, q_send, q_recv, peer).wait_recv()

            return 0

        lax.fori_loop(0, NZ, take, 0)
        attn_block(env, block, q_all, k_all, v_all, hand_all, dq_all)

        def give(i, _):
            peer = block * NZ + lax.rem(z + i, NZ)

            @pl.when(peer != me)
            def _():
                token_send(dq_all, dq_out, dq_send, dq_recv, peer).start()

            return 0

        lax.fori_loop(0, NZ, give, 0)
        return 0

    lax.fori_loop(0, NY, attend, 0)
    attn_finish(env, dk_all, dv_all)
    to_all(lambda peer: token_send(dk_all, dk_out, dk_send, dk_recv, peer).start())
    to_all(lambda peer: token_send(dv_all, dv_out, dv_send, dv_recv, peer).start())
    own = [
        token_own(dq_all, dq_out, 0),
        token_own(dk_all, dk_out, 1),
        token_own(dv_all, dv_out, 2),
    ]
    for copy in own:
        copy.start()

    for first, name in ((0, "dp_2"), (2, "dp_0"), (2 + 4, "dp_1")):
        for copy in reward_copies(first, name):
            copy.wait_send()
    for copy in (bridge_up, bridge_down, on_up, on_down, share_below, share_above, share_across):
        copy.wait_send()
    for hop in range(NZ - 1):
        vg_hop(hop, lambda copy: copy.wait_send())
    for step in range(1, NY):
        hand_copy(step).wait_send()

    def settle(peer):
        head_send(k_hbm, k_all, k_send, k_recv, peer).wait_send()
        head_send(v_hbm, v_all, v_send, v_recv, peer).wait_send()
        head_send(q_hbm, q_all, q_send, q_recv, peer).wait_send()
        token_send(dq_all, dq_out, dq_send, dq_recv, peer).wait_send()
        token_send(dk_all, dk_out, dk_send, dk_recv, peer).wait_send()
        token_send(dv_all, dv_out, dv_send, dv_recv, peer).wait_send()
        token_recv(dq_out, dq_send, dq_recv, peer).wait_recv()
        token_recv(dk_out, dk_send, dk_recv, peer).wait_recv()
        token_recv(dv_out, dv_send, dv_recv, peer).wait_recv()

    to_all(settle)
    for copy in own:
        copy.wait()


def local(
    rm_hidden, rm_cotangent, rm_gain, rewards, visual_pos, bridge, img_query, img_key, img_value
):
    sizes = tuple(lax.axis_size(a) for a in DP)
    rows, depth = rm_hidden.shape[1:]
    count = visual_pos.shape[1]
    tokens = jax.ShapeDtypeStruct(img_query.shape[1:], BF)
    anywhere = pl.BlockSpec(memory_space=pl.ANY)
    in_vmem = pl.BlockSpec(memory_space=pltpu.VMEM)
    group = pltpu.SemaphoreType.DMA((TP,))
    head = pltpu.VMEM((SEQ, HD), BF)
    grads = pl.pallas_call(
        functools.partial(kernel, sizes),
        out_shape=[tokens] * 3,
        in_specs=[pl.BlockSpec(memory_space=pltpu.SMEM), in_vmem, in_vmem] + [anywhere] * 6,
        out_specs=[anywhere] * 3,
        scratch_shapes=[
            pltpu.VMEM((rows, depth), BF),
            pltpu.VMEM((rows, depth), BF),
            pltpu.VMEM((NZ * count, depth), BF),
            pltpu.VMEM((depth, NY * HD), BF),
            pltpu.VMEM((NY, UB, HD), BF),
            pltpu.VMEM((VIS, HD), BF),
            *([head] * 6),
            pltpu.VMEM((2 + 4 + 4, 8, HD), F32),
            pltpu.SemaphoreType.DMA((6,)),
            pltpu.SemaphoreType.DMA((10,)),
            pltpu.SemaphoreType.DMA((10,)),
            pltpu.SemaphoreType.DMA((2 * NZ,)),
            pltpu.SemaphoreType.DMA((2 * NZ,)),
            pltpu.SemaphoreType.DMA((7,)),
            pltpu.SemaphoreType.DMA((7,)),
            pltpu.SemaphoreType.DMA((NY,)),
            pltpu.SemaphoreType.DMA((NY,)),
            *([group] * 12),
            *attn_scratch(),
        ],
        compiler_params=pltpu.CompilerParams(
            collective_id=0, has_side_effects=True, vmem_limit_bytes=48 << 20
        ),
    )(
        rewards,
        visual_pos,
        rm_gain[None],
        rm_hidden[0],
        rm_cotangent[0],
        bridge,
        img_query[0],
        img_key[0],
        img_value[0],
    )
    return tuple(grad[None] for grad in grads)


def solution(mesh):
    torus = Mesh(
        mesh.devices.reshape(4, 4, 2, mesh.shape["tensor"]), ("dp_0", "dp_1", "dp_2", "tensor")
    )
    return on_torus(torus)


def on_torus(torus):
    in_specs = (
        P(DP, "tensor", None),
        P(DP, "tensor", None),
        P(),
        P(DP),
        P(DP, "tensor"),
        P(None, "tensor"),
        P(DP, "tensor", None),
        P(DP, "tensor", None),
        P(DP, "tensor", None),
    )
    out_specs = (P(DP, "tensor", None), P(DP, "tensor", None), P(DP, "tensor", None))
    return jax.shard_map(local, mesh=torus, in_specs=in_specs, out_specs=out_specs, check_vma=False)
```

time: 270 us -> 128 us (0.47)
  Pallas kernels: 0 us -> 117 us
  waiting for transfers between devices: 92 us -> 0 us
  blocking collectives: 55.7 us -> 0 us
  matrix products: 41.8 us -> 0 us
  starting transfers between devices: 24.7 us -> 0 us
  between operations: 15.6 us -> 1.32 us
  other arithmetic: 13.8 us -> 0 us
  local copies, waits for them, and re-layouts: 21.7 us -> 9.45 us
  loops' own time: 2.84 us -> 0 us
    pallas_call x0 -> x1, Pallas kernels: none -> 117 us  [local(): pl.pallas_call(functools.partial(kernel, sizes), out_shape=[tokens] * 3,...]
    all_to_all x5 -> x0, waiting for transfers between devices: 71 us -> none  [the longest x1 29.3 us: local(): lax.all_to_all(img_value[0], 'tensor', split_axis=1, concat_axis=0, tiled...]
    dot_general x21 -> x0, matrix products: 41.8 us -> none  [the longest x4 19 us: step(): jnp.dot(weights_half.T, grad_block, preferred_element_type=jnp.float32)]
    psum x3 -> x0, blocking collectives: 37.6 us -> none  [one_axis_at_a_time(): return functools.reduce(lax.psum, axes, array)]
    all_to_all x5 -> x0, starting transfers between devices: 24.7 us -> none  [the longest x1 8.64 us: local(): lax.all_to_all(img_query[0], 'tensor', split_axis=1, concat_axis=0, tiled...]
    all_gather x1 -> x0, waiting for transfers between devices: 21 us -> none  [local(): lax.all_gather(visual_grad, 'tensor', axis=0, tiled=True)]
    all_to_all x1 -> x0, blocking collectives: 18.2 us -> none  [local(): lax.all_to_all(head_grads[2], 'tensor', split_axis=0, concat_axis=1, tile...]
    convert_element_type x7 -> x0, other arithmetic: 8.69 us -> none  [the longest x4 5.6 us: step(): grad_scores = (attn_weights * (grad_weights - row_dot)).astype(jnp.bfloat16)]
  transfers between devices with their start and end apart: 6 -> 0, of which waited for: 5 -> 0; matrix products, arithmetic and copies ran while one was open for 4% -> 0% of each run, Pallas kernels for 0% -> 0%
where the time goes in v1:
time: 128 us
  Pallas kernels  117 us (91%)
  local copies, waits for them, and re-layouts  9.45 us (7%)
  between operations  1.32 us (1%)
    pallas_call x1, Pallas kernels, local(): pl.pallas_call(functools.partial(kernel, sizes), out_shape=[tokens] * 3,...  117 us
    unnamed x17, local copies, waits for them, and re-layouts  8.72 us

profile of v1, /device:TPU:6, one launch (start us, length us, event | category | flops | bytes accessed | tf_op | source)
XLA Modules:
  0.0 127.9 jit_solution(572068596199402017)
XLA Ops:
  1.3 0.0 copy-start.6
  1.3 0.7 broadcast_in_dim.12.gain_ref
  2.0 0.0 copy-done.6
  2.0 0.0 copy-start
  2.0 1.2 copy-done
  3.2 0.0 copy-start.1
  3.2 1.0 copy-done.1
  4.3 0.0 copy-start.2
  4.3 1.0 copy-done.2
  5.3 0.0 copy-start.3
  5.3 1.0 copy-done.3
  6.3 0.0 copy-start.4
  6.3 1.0 copy-done.4
  7.4 0.0 copy-start.5
  7.4 1.0 copy-done.5
  8.4 117.1 %shard_map.112 = (bf16[128,2048]{1,0:T(8,128)(2,1)S(1)}, bf16[128,2048]{1,0:T(8,128)(2,1)S(1)}, bf16[128,2048]{1,0:T(8,128)(2,1)S(1)}) custom-call(f32[1]{0:T(128)S(6)} %copy.15.rew_ref, s32[1,32]{1,0:T(1,128)S(1)} %copy-done.6, f32[1,3584]{1,0:T(1,128)S(1)} %broadcast_in_dim.12.gain_ref, bf16[64,3584]{1,0:T(8,128)(2,1)S(1)} %bitcast.14, ...), custom_call_target="tpu_custom_call" | custom-call | tf_op jit(solution)/shard_map/pallas_call | solution.py:548
  125.5 0.8 copy.16
  126.3 0.8 copy.17
  127.1 0.8 copy.18
Async XLA Ops:
  1.3 0.7 copy-start.6
  2.0 1.2 copy-start
  3.2 1.0 copy-start.1
  4.3 1.0 copy-start.2
  5.3 1.0 copy-start.3
  6.3 1.0 copy-start.4
  7.4 1.0 copy-start.5

commit v2 on v1

--- a/solution.py
+++ b/solution.py
@@ -21,6 +21,7 @@
 UB = QB // 4
 KC = 256
 SCALE = HD**-0.5
+DOSES = (3, 3, 7, 11, 15, 15, 45)
 LOG2E = 1.4426950408889634
 BF = jnp.bfloat16
 F32 = jnp.float32
@@ -342,7 +343,26 @@
 
         lax.fori_loop(1, TP, one, 0)
 
-    to_all(lambda peer: head_send(k_hbm, k_all, k_send, k_recv, peer).start())
+    heads = (
+        (k_hbm, k_all, k_send, k_recv),
+        (v_hbm, v_all, v_send, v_recv),
+        (q_hbm, q_all, q_send, q_recv),
+    )
+    moved = [0]
+
+    def move_heads(until):
+        while moved[0] < until:
+            which, first = divmod(moved[0], TP - 1)
+            last = min(TP - 1, first + until - moved[0])
+
+            def one(step, _, refs=heads[which]):
+                head_send(*refs, peer_at(step)).start()
+                return 0
+
+            lax.fori_loop(first + 1, last + 1, one, 0)
+            moved[0] += last - first
+
+    move_heads(DOSES[0])
 
     local[0].wait()
     local[1].wait()
@@ -352,7 +372,7 @@
     )
     picked = picked.astype(F32).astype(BF)
     hidden = mm(picked, hid[...], TN)
-    scaled = mm(picked, cot[...], TN) * gain_ref[...]
+    scaled = mm(picked, cot[...], TN) * gain_ref[...].reshape(1, gain_ref.shape[0])
     inv_rms = lax.rsqrt(jnp.mean(hidden * hidden, axis=-1, keepdims=True) + 1e-06)
     mixed = jnp.mean(hidden * scaled, axis=-1, keepdims=True)
     count = local_rows.shape[1]
@@ -386,14 +406,14 @@
             vg_copy(lax.rem(z + hop + 1, NZ), NZ + hop, right).wait_recv()
 
     vg_hop(0, lambda copy: copy.start())
-    to_all(lambda peer: head_send(v_hbm, v_all, v_send, v_recv, peer).start())
+    move_heads(DOSES[1])
     core_total = reward_sum(0, "dp_2")
     reward_start(2, "dp_0", core_total)
     attn_tables(env)
 
     vg_take(0)
     vg_hop(1, lambda copy: copy.start())
-    to_all(lambda peer: head_send(q_hbm, q_all, q_send, q_recv, peer).start())
+    move_heads(DOSES[2])
     x_total = reward_sum(2, "dp_0")
     reward_start(2 + 4, "dp_1", x_total)
 
@@ -408,14 +428,18 @@
     on_down.start()
     share_above = bridge_copy(above, core * half, half, 5, sibling)
     share_above.start()
+    move_heads(DOSES[3])
     vg_take(1)
     vg_hop(2, lambda copy: copy.start())
+    move_heads(DOSES[4])
     bridge_copy(across, core * half, quarter, 2, down).wait_recv()
     bridge_copy(across, core * half + quarter, quarter, 3, up).wait_recv()
     share_across = bridge_copy(across, core * half, half, 6, sibling)
     share_across.start()
     other = (1 - core) * half
+    move_heads(DOSES[5])
     vg_take(2)
+    move_heads(DOSES[6])
     z_total = reward_sum(2 + 4, "dp_1")
     weight = rew_ref[0] * (n_x * n_zhi * n_core) / z_total[0:1, :]
 
@@ -541,7 +565,7 @@
     rows, depth = rm_hidden.shape[1:]
     count = visual_pos.shape[1]
     tokens = jax.ShapeDtypeStruct(img_query.shape[1:], BF)
-    anywhere = pl.BlockSpec(memory_space=pl.ANY)
+    anywhere = pl.BlockSpec(memory_space=pltpu.HBM)
     in_vmem = pl.BlockSpec(memory_space=pltpu.VMEM)
     group = pltpu.SemaphoreType.DMA((TP,))
     head = pltpu.VMEM((SEQ, HD), BF)
@@ -572,12 +596,12 @@
             *attn_scratch(),
         ],
         compiler_params=pltpu.CompilerParams(
-            collective_id=0, has_side_effects=True, vmem_limit_bytes=48 << 20
+            collective_id=0, has_side_effects=True, vmem_limit_bytes=63 << 20
         ),
     )(
         rewards,
         visual_pos,
-        rm_gain[None],
+        rm_gain,
         rm_hidden[0],
         rm_cotangent[0],
         bridge,

time: 128 us -> 114 us (0.89)
  Pallas kernels: 117 us -> 109 us
  local copies, waits for them, and re-layouts: 9.45 us -> 3.97 us
    pallas_call x1, Pallas kernels: 117 us -> 109 us  [local(): pl.pallas_call(functools.partial(kernel, sizes), out_shape=[tokens] * 3,...]
    unnamed x17 -> x7, local copies, waits for them, and re-layouts: 8.72 us -> 3.97 us
where the time goes in v2:
time: 114 us
  Pallas kernels  109 us (96%)
  local copies, waits for them, and re-layouts  3.97 us (3%)
  between operations  1.3 us (1%)
    pallas_call x1, Pallas kernels, local(): pl.pallas_call(functools.partial(kernel, sizes), out_shape=[tokens] * 3,...  109 us
    unnamed x7, local copies, waits for them, and re-layouts  3.97 us

profile of v2, /device:TPU:6, one launch (start us, length us, event | category | flops | bytes accessed | tf_op | source)
XLA Modules:
  0.0 113.9 jit_solution(6410076892400873389)
XLA Ops:
  1.3 108.6 %shard_map.112 = (bf16[128,2048]{1,0:T(8,128)(2,1)}, bf16[128,2048]{1,0:T(8,128)(2,1)}, bf16[128,2048]{1,0:T(8,128)(2,1)}) custom-call(f32[1]{0:T(128)S(6)} %copy.15.rew_ref, s32[1,32]{1,0:T(1,128)} %pos_ref.1, f32[3584]{0:T(1024)} %gain_ref.1, bf16[64,3584]{1,0:T(8,128)(2,1)} %bitcast.14, bf16[64,3584]{1,0:T(8,128)(2,1)} %bitcast.15, ...), custom_call_target="tpu_custom_call" | custom-call | tf_op jit(solution)/shard_map/pallas_call | solution.py:572
  109.9 0.0 copy-start.1
  109.9 1.9 %copy.16 = bf16[1,128,2048]{2,1,0:T(8,128)(2,1)} copy(bf16[1,128,2048]{2,1,0:T(8,128)(2,1)} %bitcast.13) | data formatting | bytes 1048576
  111.8 0.0 copy-done.1
  111.8 0.0 copy-start
  111.8 0.8 copy.17
  112.6 0.4 copy-done
  113.1 0.8 copy.18
Async XLA Ops:
  109.9 2.0 %copy-start.1 = (bf16[128,2048]{1,0:T(8,128)(2,1)S(1)}, bf16[128,2048]{1,0:T(8,128)(2,1)}, u32[]{:S(2)}) copy-start(bf16[128,2048]{1,0:T(8,128)(2,1)} %get-tuple-element.7) | copy-start | bytes 1572868
  111.8 1.2 %copy-start = (bf16[128,2048]{1,0:T(8,128)(2,1)S(1)}, bf16[128,2048]{1,0:T(8,128)(2,1)}, u32[]{:S(2)}) copy-start(bf16[128,2048]{1,0:T(8,128)(2,1)} %get-tuple-element.8) | copy-start | bytes 1572868

commit v3 on v2

--- a/solution.py
+++ b/solution.py
@@ -94,7 +94,7 @@
     return jnp.concatenate([values] * 4, axis=1)
 
 
-def attn_block(env, block, q_all, k_all, v_all, hand_all, dq_all):
+def attn_block(env, block, q_all, k_all, v_all, hand_all):
     q_rows = pl.ds(pl.multiple_of(block * QB, QB), QB)
     q_g = mm(env.perm[...], q_all[q_rows, :]).astype(BF)
     hand = hand_all[pl.ds(pl.multiple_of(block * UB, UB), UB), :]
@@ -134,21 +134,17 @@
         return 0
 
     lax.fori_loop(0, SEQ // KC, grads, 0, unroll=2)
-    dq_t = (env.dq_t[...] * SCALE).astype(BF)
+
+
+def attn_close(env, block, dq_all, weight):
+    q_rows = pl.ds(pl.multiple_of(block * QB, QB), QB)
+    dq_t = (env.dq_t[...] * four(weight * SCALE)).astype(BF)
     dq_all[q_rows, :] = mm(env.perm_t[...], dq_t, NT).astype(BF)
 
 
-def attn_finish(env, dk_all, dv_all):
-    dk_all[...] = (env.dk_acc[...] * SCALE).astype(BF)
-    dv_all[...] = env.dv_acc[...].astype(BF)
-
-
-class Links(NamedTuple):
-    x: Any
-    z_hi: Any
-    core: Any
-    tensor: Any
-    sizes: tuple
+def attn_finish(env, dk_all, dv_all, weight):
+    dk_all[...] = (env.dk_acc[...] * (weight * SCALE)).astype(BF)
+    dv_all[...] = (env.dv_acc[...] * weight).astype(BF)
 
 
 def remote(src, dst, send_sem, recv_sem, device):
@@ -189,9 +185,15 @@
     dk_all,
     dv_all,
     rew,
+    total,
     own_sem,
-    rew_send,
-    rew_recv,
+    group_sem,
+    pair_send,
+    pair_recv,
+    lead_send,
+    lead_recv,
+    total_send,
+    total_recv,
     vg_send,
     vg_recv,
     br_send,
@@ -223,24 +225,44 @@
         return {name: lax.rem(place + step, size)}
 
     barrier = pltpu.get_barrier_semaphore()
+    first = me == 0
+    lead, second = first & (core == 0), first & (core == 1)
+    n_leads = n_x * n_zhi
+    lead_at = x * n_zhi + z_hi
+
+    def signal(semaphore, device):
+        pl.semaphore_signal(
+            semaphore, inc=1, device_id=device, device_id_type=pl.DeviceIdType.MESH
+        )
+
+    def lead_device(step):
+        place = lax.rem(lead_at + step, n_leads)
+        return {"dp_0": place // n_zhi, "dp_1": lax.rem(place, n_zhi)}
+
+    sibling = turned("dp_2", 1)
 
     def greet(step, _):
-        pl.semaphore_signal(
-            barrier,
-            inc=1,
-            device_id={"tensor": lax.rem(me + step, TP)},
-            device_id_type=pl.DeviceIdType.MESH,
-        )
+        peer = lax.rem(me + step, TP)
+
+        @pl.when((peer != 0) | (core == 1))
+        def _():
+            signal(barrier, {"tensor": peer})
+
         return 0
 
     lax.fori_loop(1, TP, greet, 0)
-    partners = TP - 1
-    for name, (_, size) in axis_of.items():
-        for step in range(1, size):
-            pl.semaphore_signal(
-                barrier, inc=1, device_id=turned(name, step), device_id_type=pl.DeviceIdType.MESH
-            )
-            partners += 1
+
+    @pl.when(~second)
+    def _():
+        signal(barrier, sibling)
+
+    @pl.when(lead)
+    def _():
+        def greet_lead(step, _):
+            signal(barrier, lead_device(step))
+            return 0
+
+        lax.fori_loop(1, n_leads, greet_lead, 0)
 
     mine = pl.ds(pl.multiple_of(me * HD, HD), HD)
     my_cols = pl.ds(pl.multiple_of(y * HD, HD), HD)
@@ -254,44 +276,79 @@
     ]
     for copy in local:
         copy.start()
-    pl.semaphore_wait(barrier, partners)
-
-    def reward_copies(first, name):
-        place, size = axis_of[name]
-        return [
-            remote(
-                rew.at[first + place],
-                rew.at[first + place],
-                rew_send.at[first + step],
-                rew_recv.at[first + place],
-                turned(name, step),
-            )
-            for step in range(1, size)
-        ]
-
-    def reward_start(first, name, value):
-        rew[first + axis_of[name][0]] = value
-        for copy in reward_copies(first, name):
-            copy.start()
-
-    def reward_sum(first, name):
-        place, size = axis_of[name]
-        for step in range(1, size):
-            other = lax.rem(place + step, size)
-            remote(
-                rew.at[first + other],
-                rew.at[first + other],
-                rew_send.at[first + step],
-                rew_recv.at[first + other],
-                turned(name, step),
-            ).wait_recv()
-        total = rew[first]
-        for slot in range(1, size):
-            total = total + rew[first + slot]
-        return total
+    @pl.when(~lead)
+    def _():
+        pl.semaphore_wait(barrier, TP)
+
+    @pl.when((~first) & (core == 0))
+    def _():
+        signal(group_sem, {"tensor": 0})
+
+    @pl.when(second)
+    def _():
+        signal(group_sem, sibling)
+
+    @pl.when(lead)
+    def _():
+        pl.semaphore_wait(group_sem, TP)
 
     my_reward = jnp.full((8, HD), rew_ref[0], F32)
-    reward_start(0, "dp_2", my_reward)
+
+    def pair_copy():
+        return remote(rew.at[n_leads], rew.at[n_leads], pair_send, pair_recv, sibling)
+
+    def lead_copy(step):
+        slot = rew.at[lead_at]
+        return remote(slot, slot, lead_send.at[step], lead_recv.at[lead_at], lead_device(step))
+
+    def total_copy(slot, device):
+        return remote(total, total, total_send.at[slot], total_recv, device)
+
+    def each(count, action):
+        def one(step, _):
+            action(step)
+            return 0
+
+        lax.fori_loop(1, count, one, 0)
+
+    def group_copy(step):
+        return total_copy(step, {"tensor": lax.rem(me + step, TP)})
+
+    @pl.when(second)
+    def _():
+        rew[n_leads] = my_reward
+        pair_copy().start()
+
+    def rewards_out():
+        @pl.when(lead)
+        def _():
+            pl.semaphore_wait(barrier, n_leads - 1)
+            pair_copy().wait_recv()
+            rew[lead_at] = my_reward + rew[n_leads]
+            each(n_leads, lambda step: lead_copy(step).start())
+
+    def rewards_back():
+        @pl.when(lead)
+        def _():
+            def take_lead(step):
+                place = lax.rem(lead_at + step, n_leads)
+                slot = rew.at[place]
+                remote(
+                    slot, slot, lead_send.at[step], lead_recv.at[place], lead_device(step)
+                ).wait_recv()
+
+            each(n_leads, take_lead)
+            all_pairs = rew[0]
+            for place in range(1, n_leads):
+                all_pairs = all_pairs + rew[place]
+            total[...] = all_pairs
+            total_copy(0, sibling).start()
+            each(TP, lambda step: group_copy(step).start())
+
+        @pl.when(second)
+        def _():
+            total_copy(0, sibling).wait_recv()
+            each(TP, lambda step: group_copy(step).start())
 
     half, quarter = D // 2, D // 4
     up, down = {"tensor": lax.rem(y + 1, NY) * NZ + z}, {"tensor": lax.rem(y + NY - 1, NY) * NZ + z}
@@ -407,17 +464,13 @@
 
     vg_hop(0, lambda copy: copy.start())
     move_heads(DOSES[1])
-    core_total = reward_sum(0, "dp_2")
-    reward_start(2, "dp_0", core_total)
     attn_tables(env)
 
     vg_take(0)
     vg_hop(1, lambda copy: copy.start())
     move_heads(DOSES[2])
-    x_total = reward_sum(2, "dp_0")
-    reward_start(2 + 4, "dp_1", x_total)
-
-    sibling = turned("dp_2", 1)
+    rewards_out()
+
     bridge_copy(below, core * half, half, 0, down).wait_recv()
     on_up = bridge_copy(below, core * half, quarter, 2, up)
     on_up.start()
@@ -440,13 +493,11 @@
     move_heads(DOSES[5])
     vg_take(2)
     move_heads(DOSES[6])
-    z_total = reward_sum(2 + 4, "dp_1")
-    weight = rew_ref[0] * (n_x * n_zhi * n_core) / z_total[0:1, :]
 
     def hand_head(owner):
         cols = pl.ds(pl.multiple_of(owner * HD, HD), HD)
         product = mm(vg_all[...], bridge_all[:, cols])
-        return (product * weight).astype(BF)
+        return product.astype(BF)
 
     my_rows = pl.ds(pl.multiple_of(y * UB, UB), UB)
 
@@ -467,6 +518,8 @@
         bridge_copy(owner, other, half, slot, sibling).wait_recv()
         hand_mine[step] = hand_head(owner)
         hand_copy(step).start()
+
+    rewards_back()
 
     for copy in local[3:]:
         copy.wait()
@@ -493,6 +546,9 @@
     def token_own(all_ref, out, slot):
         return pltpu.make_async_copy(all_ref.at[mine, :], out.at[:, mine], own_sem.at[slot])
 
+    def weight_of():
+        return rew_ref[0] * (n_x * n_zhi * n_core) / total[0:1, :]
+
     def attend(step, _):
         block = lax.rem(y + step, NY)
 
@@ -506,7 +562,13 @@
             return 0
 
         lax.fori_loop(0, NZ, take, 0)
-        attn_block(env, block, q_all, k_all, v_all, hand_all, dq_all)
+        attn_block(env, block, q_all, k_all, v_all, hand_all)
+
+        @pl.when((step == 0) & ~first)
+        def _():
+            group_copy(1).wait_recv()
+
+        attn_close(env, block, dq_all, weight_of())
 
         def give(i, _):
             peer = block * NZ + lax.rem(z + i, NZ)
@@ -521,7 +583,7 @@
         return 0
 
     lax.fori_loop(0, NY, attend, 0)
-    attn_finish(env, dk_all, dv_all)
+    attn_finish(env, dk_all, dv_all, weight_of())
     to_all(lambda peer: token_send(dk_all, dk_out, dk_send, dk_recv, peer).start())
     to_all(lambda peer: token_send(dv_all, dv_out, dv_send, dv_recv, peer).start())
     own = [
@@ -532,9 +594,19 @@
     for copy in own:
         copy.start()
 
-    for first, name in ((0, "dp_2"), (2, "dp_0"), (2 + 4, "dp_1")):
-        for copy in reward_copies(first, name):
-            copy.wait_send()
+    @pl.when(second)
+    def _():
+        pair_copy().wait_send()
+
+    @pl.when(lead)
+    def _():
+        each(n_leads, lambda step: lead_copy(step).wait_send())
+        total_copy(0, sibling).wait_send()
+
+    @pl.when(first)
+    def _():
+        each(TP, lambda step: group_copy(step).wait_send())
+
     for copy in (bridge_up, bridge_down, on_up, on_down, share_below, share_above, share_across):
         copy.wait_send()
     for hop in range(NZ - 1):
@@ -562,6 +634,7 @@
     rm_hidden, rm_cotangent, rm_gain, rewards, visual_pos, bridge, img_query, img_key, img_value
 ):
     sizes = tuple(lax.axis_size(a) for a in DP)
+    n_leads = sizes[0] * sizes[1]
     rows, depth = rm_hidden.shape[1:]
     count = visual_pos.shape[1]
     tokens = jax.ShapeDtypeStruct(img_query.shape[1:], BF)
@@ -582,10 +655,16 @@
             pltpu.VMEM((NY, UB, HD), BF),
             pltpu.VMEM((VIS, HD), BF),
             *([head] * 6),
-            pltpu.VMEM((2 + 4 + 4, 8, HD), F32),
+            pltpu.VMEM((n_leads + 1, 8, HD), F32),
+            pltpu.VMEM((8, HD), F32),
             pltpu.SemaphoreType.DMA((6,)),
-            pltpu.SemaphoreType.DMA((10,)),
-            pltpu.SemaphoreType.DMA((10,)),
+            pltpu.SemaphoreType.REGULAR,
+            pltpu.SemaphoreType.DMA,
+            pltpu.SemaphoreType.DMA,
+            pltpu.SemaphoreType.DMA((n_leads,)),
+            pltpu.SemaphoreType.DMA((n_leads,)),
+            group,
+            pltpu.SemaphoreType.DMA,
             pltpu.SemaphoreType.DMA((2 * NZ,)),
             pltpu.SemaphoreType.DMA((2 * NZ,)),
             pltpu.SemaphoreType.DMA((7,)),

time: 114 us -> 102 us (0.89)
  Pallas kernels: 109 us -> 96.7 us
    pallas_call x1, Pallas kernels: 109 us -> 96.7 us  [local(): pl.pallas_call(functools.partial(kernel, sizes), out_shape=[tokens] * 3,...]
where the time goes in v3:
time: 102 us
  Pallas kernels  96.7 us (95%)
  local copies, waits for them, and re-layouts  3.97 us (4%)
  between operations  1.3 us (1%)
    pallas_call x1, Pallas kernels, local(): pl.pallas_call(functools.partial(kernel, sizes), out_shape=[tokens] * 3,...  96.7 us
    unnamed x7, local copies, waits for them, and re-layouts  3.97 us

profile of v3, /device:TPU:6, one launch (start us, length us, event | category | flops | bytes accessed | tf_op | source)
XLA Modules:
  0.0 101.9 jit_solution(3374874786386379550)
XLA Ops:
  1.3 96.7 %shard_map.112 = (bf16[128,2048]{1,0:T(8,128)(2,1)}, bf16[128,2048]{1,0:T(8,128)(2,1)}, bf16[128,2048]{1,0:T(8,128)(2,1)}) custom-call(f32[1]{0:T(128)S(6)} %copy.15.rew_ref, s32[1,32]{1,0:T(1,128)} %pos_ref.1, f32[3584]{0:T(1024)} %gain_ref.1, bf16[64,3584]{1,0:T(8,128)(2,1)} %bitcast.14, bf16[64,3584]{1,0:T(8,128)(2,1)} %bitcast.15, ...), custom_call_target="tpu_custom_call" | custom-call | tf_op jit(solution)/shard_map/pallas_call | solution.py:645
  98.0 0.0 copy-start.1
  98.0 1.9 %copy.16 = bf16[1,128,2048]{2,1,0:T(8,128)(2,1)} copy(bf16[1,128,2048]{2,1,0:T(8,128)(2,1)} %bitcast.13) | data formatting | bytes 1048576
  99.9 0.0 copy-done.1
  99.9 0.0 copy-start
  99.9 0.8 copy.17
  100.7 0.4 copy-done
  101.1 0.8 copy.18
Async XLA Ops:
  98.0 2.0 %copy-start.1 = (bf16[128,2048]{1,0:T(8,128)(2,1)S(1)}, bf16[128,2048]{1,0:T(8,128)(2,1)}, u32[]{:S(2)}) copy-start(bf16[128,2048]{1,0:T(8,128)(2,1)} %get-tuple-element.7) | copy-start | bytes 1572868
  99.9 1.2 %copy-start = (bf16[128,2048]{1,0:T(8,128)(2,1)S(1)}, bf16[128,2048]{1,0:T(8,128)(2,1)}, u32[]{:S(2)}) copy-start(bf16[128,2048]{1,0:T(8,128)(2,1)} %get-tuple-element.8) | copy-start | bytes 1572868

commit v4 on v3

--- a/solution.py
+++ b/solution.py
@@ -21,7 +21,8 @@
 UB = QB // 4
 KC = 256
 SCALE = HD**-0.5
-DOSES = (3, 3, 7, 11, 15, 15, 45)
+PARTS = 2
+DOSES = (3, 3, 7, 11, 15, 15, 33)
 LOG2E = 1.4426950408889634
 BF = jnp.bfloat16
 F32 = jnp.float32
@@ -107,7 +108,7 @@
         env.s_buf[rows(chunk), :] = s
         return jnp.maximum(top, fold(s, jnp.max))
 
-    top = lax.fori_loop(0, SEQ // KC, scores, jnp.full((8, QB), -jnp.inf, F32), unroll=2)
+    top = lax.fori_loop(0, SEQ // KC, scores, jnp.full((8, QB), -jnp.inf, F32), unroll=8)
     top = jnp.max(top, axis=0, keepdims=True)
 
     def weights(chunk, carry):
@@ -119,7 +120,7 @@
         return total + fold(e, jnp.sum), dot_sum + fold(e * four(dp), jnp.sum)
 
     zeros = jnp.zeros((8, QB), F32)
-    total, dot_sum = lax.fori_loop(0, SEQ // KC, weights, (zeros, zeros), unroll=2)
+    total, dot_sum = lax.fori_loop(0, SEQ // KC, weights, (zeros, zeros), unroll=8)
     inv = 1.0 / jnp.sum(total, axis=0, keepdims=True)
     row_dot = jnp.sum(dot_sum, axis=0, keepdims=True) * inv
     env.dq_t[...] = jnp.zeros((HD, QB), F32)
@@ -133,7 +134,7 @@
         env.dq_t[...] += mm(env.k_t[:, rows(chunk)], ds)
         return 0
 
-    lax.fori_loop(0, SEQ // KC, grads, 0, unroll=2)
+    lax.fori_loop(0, SEQ // KC, grads, 0, unroll=8)
 
 
 def attn_close(env, block, dq_all, weight):
@@ -142,9 +143,8 @@
     dq_all[q_rows, :] = mm(env.perm_t[...], dq_t, NT).astype(BF)
 
 
-def attn_finish(env, dk_all, dv_all, weight):
-    dk_all[...] = (env.dk_acc[...] * (weight * SCALE)).astype(BF)
-    dv_all[...] = (env.dv_acc[...] * weight).astype(BF)
+def attn_finish(acc, out, weight):
+    out[...] = (acc[...] * weight).astype(BF)
 
 
 def remote(src, dst, send_sem, recv_sem, device):
@@ -437,37 +437,46 @@
         inv_rms * scaled - hidden * (inv_rms * inv_rms * inv_rms * mixed)
     ).astype(BF)
 
-    def vg_copy(owner, slot, device):
-        region = vg_all.at[pl.ds(pl.multiple_of(owner * count, count), count), :]
+    part = count // PARTS
+
+    def vg_copy(owner, slot, device, at):
+        region = vg_all.at[pl.ds(pl.multiple_of(owner * count + at * part, part), part), :]
+        slot = at * 2 * NZ + slot
         return remote(region, region, vg_send.at[slot], vg_recv.at[slot], device)
 
     right = {"tensor": y * NZ + lax.rem(z + 1, NZ)}
     left = {"tensor": y * NZ + lax.rem(z + NZ - 1, NZ)}
 
-    def vg_hop(hop, action):
+    def vg_hop(hop, at, action):
         @pl.when((z < NZ - 1) & (z >= hop))
         def _():
-            action(vg_copy(lax.rem(z - hop + NZ, NZ), hop, right))
+            action(vg_copy(lax.rem(z - hop + NZ, NZ), hop, right, at))
 
         @pl.when((z > 0) & (z + hop < NZ))
         def _():
-            action(vg_copy(lax.rem(z + hop, NZ), NZ + hop, left))
-
-    def vg_take(hop):
+            action(vg_copy(lax.rem(z + hop, NZ), NZ + hop, left, at))
+
+    def vg_take(hop, at):
         @pl.when(z > hop)
         def _():
-            vg_copy(lax.rem(z - hop - 1 + NZ, NZ), hop, left).wait_recv()
+            vg_copy(lax.rem(z - hop - 1 + NZ, NZ), hop, left, at).wait_recv()
 
         @pl.when(z + hop + 1 < NZ)
         def _():
-            vg_copy(lax.rem(z + hop + 1, NZ), NZ + hop, right).wait_recv()
-
-    vg_hop(0, lambda copy: copy.start())
+            vg_copy(lax.rem(z + hop + 1, NZ), NZ + hop, right, at).wait_recv()
+
+    def vg_on(hop):
+        for at in range(PARTS):
+            vg_take(hop, at)
+            if hop + 1 < NZ - 1:
+                vg_hop(hop + 1, at, lambda copy: copy.start())
+
+    for at in range(PARTS):
+        vg_hop(0, at, lambda copy: copy.start())
     move_heads(DOSES[1])
     attn_tables(env)
 
-    vg_take(0)
-    vg_hop(1, lambda copy: copy.start())
+    vg_on(0)
     move_heads(DOSES[2])
     rewards_out()
 
@@ -482,8 +491,7 @@
     share_above = bridge_copy(above, core * half, half, 5, sibling)
     share_above.start()
     move_heads(DOSES[3])
-    vg_take(1)
-    vg_hop(2, lambda copy: copy.start())
+    vg_on(1)
     move_heads(DOSES[4])
     bridge_copy(across, core * half, quarter, 2, down).wait_recv()
     bridge_copy(across, core * half + quarter, quarter, 3, up).wait_recv()
@@ -491,7 +499,7 @@
     share_across.start()
     other = (1 - core) * half
     move_heads(DOSES[5])
-    vg_take(2)
+    vg_on(2)
     move_heads(DOSES[6])
 
     def hand_head(owner):
@@ -552,6 +560,14 @@
     def attend(step, _):
         block = lax.rem(y + step, NY)
 
+        @pl.when(step < NY - 1)
+        def _():
+            def ask(i, _):
+                head_send(q_hbm, q_all, q_send, q_recv, peer_at((step + 1) * NZ + i)).start()
+                return 0
+
+            lax.fori_loop(0, NZ, ask, 0)
+
         def take(i, _):
             peer = block * NZ + i
 
@@ -583,8 +599,9 @@
         return 0
 
     lax.fori_loop(0, NY, attend, 0)
-    attn_finish(env, dk_all, dv_all, weight_of())
+    attn_finish(env.dk_acc, dk_all, weight_of() * SCALE)
     to_all(lambda peer: token_send(dk_all, dk_out, dk_send, dk_recv, peer).start())
+    attn_finish(env.dv_acc, dv_all, weight_of())
     to_all(lambda peer: token_send(dv_all, dv_out, dv_send, dv_recv, peer).start())
     own = [
         token_own(dq_all, dq_out, 0),
@@ -610,7 +627,8 @@
     for copy in (bridge_up, bridge_down, on_up, on_down, share_below, share_above, share_across):
         copy.wait_send()
     for hop in range(NZ - 1):
-        vg_hop(hop, lambda copy: copy.wait_send())
+        for at in range(PARTS):
+            vg_hop(hop, at, lambda copy: copy.wait_send())
     for step in range(1, NY):
         hand_copy(step).wait_send()
 
@@ -665,8 +683,8 @@
             pltpu.SemaphoreType.DMA((n_leads,)),
             group,
             pltpu.SemaphoreType.DMA,
-            pltpu.SemaphoreType.DMA((2 * NZ,)),
-            pltpu.SemaphoreType.DMA((2 * NZ,)),
+            pltpu.SemaphoreType.DMA((2 * NZ * PARTS,)),
+            pltpu.SemaphoreType.DMA((2 * NZ * PARTS,)),
             pltpu.SemaphoreType.DMA((7,)),
             pltpu.SemaphoreType.DMA((7,)),
             pltpu.SemaphoreType.DMA((NY,)),
@@ -688,7 +706,39 @@
         img_key[0],
         img_value[0],
     )
-    return tuple(grad[None] for grad in grads)
+    settled = pl.pallas_call(
+        settle_copies,
+        out_shape=[tokens] * 3,
+        in_specs=[anywhere] * 3,
+        out_specs=[anywhere] * 3,
+        scratch_shapes=[
+            pltpu.VMEM((3, *tokens.shape), BF),
+            pltpu.SemaphoreType.DMA((3, 4)),
+            pltpu.SemaphoreType.DMA((3, 4)),
+        ],
+    )(*grads)
+    return tuple(grad[None] for grad in settled)
+
+
+def settle_copies(*refs):
+    held, came, went = refs[6:]
+    part = held.shape[1] // 4
+    pieces = [(i, k, pl.ds(k * part, part)) for i in range(3) for k in range(4)]
+    into = [
+        pltpu.make_async_copy(refs[i].at[rows, :], held.at[i, rows, :], came.at[i, k])
+        for i, k, rows in pieces
+    ]
+    out = [
+        pltpu.make_async_copy(held.at[i, rows, :], refs[i + 3].at[rows, :], went.at[i, k])
+        for i, k, rows in pieces
+    ]
+    for copy in into:
+        copy.start()
+    for arrived, copy in zip(into, out):
+        arrived.wait()
+        copy.start()
+    for copy in out:
+        copy.wait()
 
 
 def solution(mesh):

time: 102 us -> 98.6 us (0.967); the launches traced: 102 us -> 96.7 us
  local copies, waits for them, and re-layouts: 3.97 us -> 0 us
  Pallas kernels: 96.7 us -> 95.4 us
    unnamed x7 -> x0, local copies, waits for them, and re-layouts: 3.97 us -> none
    pallas_call x1, Pallas kernels: 96.7 us -> 93.1 us  [local(): pl.pallas_call(functools.partial(kernel, sizes), out_shape=[tokens] * 3,...]
    pallas_call x0 -> x1, Pallas kernels: none -> 2.33 us  [local(): pl.pallas_call(settle_copies, out_shape=[tokens] * 3, in_specs=[anywhere]...]
where the time goes in v4:
time: 98.6 us; the launch traced here: 96.7 us
  Pallas kernels  95.4 us (97%)
  between operations  1.29 us (1%)
    pallas_call x1, Pallas kernels, local(): pl.pallas_call(functools.partial(kernel, sizes), out_shape=[tokens] * 3,...  93.1 us
    pallas_call x1, Pallas kernels, local(): pl.pallas_call(settle_copies, out_shape=[tokens] * 3, in_specs=[anywhere]...  2.33 us

profile of v4, /device:TPU:6, one launch (start us, length us, event | category | flops | bytes accessed | tf_op | source)
XLA Modules:
  0.0 96.7 jit_solution(15709830623548579172)
XLA Ops:
  1.3 93.1 %shard_map.112 = (bf16[128,2048]{1,0:T(8,128)(2,1)}, bf16[128,2048]{1,0:T(8,128)(2,1)}, bf16[128,2048]{1,0:T(8,128)(2,1)}) custom-call(f32[1]{0:T(128)S(6)} %copy.12.rew_ref, s32[1,32]{1,0:T(1,128)} %pos_ref.1, f32[3584]{0:T(1024)} %gain_ref.1, bf16[64,3584]{1,0:T(8,128)(2,1)} %bitcast.11, bf16[64,3584]{1,0:T(8,128)(2,1)} %bitcast.12, ...), custom_call_target="tpu_custom_call" | custom-call | tf_op jit(solution)/shard_map/pallas_call | solution.py:663
  94.4 2.3 %shard_map.113 = (bf16[128,2048]{1,0:T(8,128)(2,1)}, bf16[128,2048]{1,0:T(8,128)(2,1)}, bf16[128,2048]{1,0:T(8,128)(2,1)}) custom-call(bf16[128,2048]{1,0:T(8,128)(2,1)} %get-tuple-element.9.refs_0_, bf16[128,2048]{1,0:T(8,128)(2,1)} %get-tuple-element.10.refs_1_, bf16[128,2048]{1,0:T(8,128)(2,1)} %get-tuple-element.11.refs_2_), custom_call_target="tpu_custom_call" | custom-call | tf_op jit(solution)/shard_map/pallas_call | solution.py:709

commit v5 on v4

--- a/solution.py
+++ b/solution.py
@@ -395,7 +395,7 @@
 
     def to_all(copy_to):
         def one(step, _):
-            copy_to(peer_at(step))
+            copy_to(peer_at(lax.rem(step, NY) * NZ + step // NY))
             return 0
 
         lax.fori_loop(1, TP, one, 0)
@@ -476,10 +476,9 @@
     move_heads(DOSES[1])
     attn_tables(env)
 
+    rewards_out()
     vg_on(0)
     move_heads(DOSES[2])
-    rewards_out()
-
     bridge_copy(below, core * half, half, 0, down).wait_recv()
     on_up = bridge_copy(below, core * half, quarter, 2, up)
     on_up.start()

time: 98.6 us -> 97.7 us (level)
  the two profiles are of different devices: /device:TPU:6 before, /device:TPU:40 now
where the time goes in v5:
time: 97.7 us; the launch traced here: 97.5 us
  Pallas kernels  96.2 us (98%)
  between operations  1.29 us (1%)
    pallas_call x1, Pallas kernels, local(): pl.pallas_call(functools.partial(kernel, sizes), out_shape=[tokens] * 3,...  93.9 us
    pallas_call x1, Pallas kernels, local(): pl.pallas_call(settle_copies, out_shape=[tokens] * 3, in_specs=[anywhere]...  2.33 us

profile of v5, /device:TPU:40, one launch (start us, length us, event | category | flops | bytes accessed | tf_op | source)
XLA Modules:
  0.0 97.5 jit_solution(5643414409131690589)
XLA Ops:
  1.3 93.9 %shard_map.112 = (bf16[128,2048]{1,0:T(8,128)(2,1)}, bf16[128,2048]{1,0:T(8,128)(2,1)}, bf16[128,2048]{1,0:T(8,128)(2,1)}) custom-call(f32[1]{0:T(128)S(6)} %copy.12.rew_ref, s32[1,32]{1,0:T(1,128)} %pos_ref.1, f32[3584]{0:T(1024)} %gain_ref.1, bf16[64,3584]{1,0:T(8,128)(2,1)} %bitcast.11, bf16[64,3584]{1,0:T(8,128)(2,1)} %bitcast.12, ...), custom_call_target="tpu_custom_call" | custom-call | tf_op jit(solution)/shard_map/pallas_call | solution.py:662
  95.2 2.3 %shard_map.113 = (bf16[128,2048]{1,0:T(8,128)(2,1)}, bf16[128,2048]{1,0:T(8,128)(2,1)}, bf16[128,2048]{1,0:T(8,128)(2,1)}) custom-call(bf16[128,2048]{1,0:T(8,128)(2,1)} %get-tuple-element.9.refs_0_, bf16[128,2048]{1,0:T(8,128)(2,1)} %get-tuple-element.10.refs_1_, bf16[128,2048]{1,0:T(8,128)(2,1)} %get-tuple-element.11.refs_2_), custom_call_target="tpu_custom_call" | custom-call | tf_op jit(solution)/shard_map/pallas_call | solution.py:708
